TPU v7x, 256 devices: a whole 4x4x8 slice. The times are simulated.
256 devices in a mesh: cp: 32 (over z_lo, y, core), tp: 8 (over z_hi, x).
Axes of the slice: x: 4, y: 4, z: 8 (z_hi: 2, z_lo: 4; z = z_hi * 4 + z_lo), core: 2. Of those that a mesh axis runs over, the one named last changes fastest.
Arguments:
- tokens: bfloat16 [16384, 4096], P('cp', 'tp'), may hold values from -40 to 40
- span_ids: int32 [32, 2], P('cp'), may hold values from 0 to 63, as said below
- positions: int32 [16384], P('cp'), may hold values from 0 to 8191, as said below
- q_weight: bfloat16 [4096, 4096], P(None, 'tp'), may hold values from -0.09375 to 0.09375
- k_weight: bfloat16 [4096, 1024], P(None, 'tp'), may hold values from -0.09375 to 0.09375
- v_weight: bfloat16 [4096, 1024], P(None, 'tp'), may hold values from -0.09375 to 0.09375
- o_weight: bfloat16 [4096, 4096], P('tp'), may hold values from -0.09375 to 0.09375
Outputs:
- attended: bfloat16 [16384, 4096], P('cp', 'tp')
Inputs may be any that keep to these rules, and one draw needn't show every extreme that they name: `span_ids`: row r names the two spans held by index r of cp: a span c and the span 64 - 1 - c, in either order; every span is named once. Span c covers the places c * (256) to (c + 1) * 256 - 1 of the sequence. `positions`: along the sequence (in the order of places given by span_ids) documents are runs of consecutive tokens; a position is 0 at a document's first token and rises by one up to its last, and the first place of the sequence has position 0.
All inputs are finite; a program needn't handle non-finite values.
Results may differ from a plain program's by a relative error of at most 0.014.
The roundings to bfloat16 on the way count: a program that leaves them out, or rounds other values in their place, can miss the bound.
Values may be sent and summed in bfloat16 or wider, within the bound.
A program may use at most 64 MiB of HBM per device.

v0:
```python
from functools import partial

import jax
import jax.numpy as jnp
from jax import lax
from jax.sharding import Mesh
from jax.sharding import PartitionSpec as P

HD = 128
TP = ("tp_0", "tp_1")
CP = ("cp_0", "cp_1", "cp_2")


theta_base = 500000.0
floor_score = -1e30


def in_order(pieces, dim):
    shape = list(pieces.shape[1:])
    shape[dim] *= pieces.shape[0]
    return jnp.moveaxis(pieces, 0, dim).reshape(shape)


def all_blocks(value, axes, order):
    pieces = value[None]
    for k in order:
        pieces = lax.all_gather(pieces, axes[k], axis=0, tiled=True)
    current = [lax.axis_size(axes[k]) for k in reversed(order)]
    pieces = pieces.reshape(*current, *value.shape)
    turned = sorted(range(len(order)), key=lambda place: order[len(order) - 1 - place])
    return pieces.transpose(*turned, *range(len(order), pieces.ndim)).reshape(-1, *value.shape)


def gather_axes(value, axes, order, dim):
    return in_order(all_blocks(value, axes, order), dim)


def from_behind(block, axis, distance):
    devices = range(lax.axis_size(axis))
    route = [((i - distance) % len(devices), i) for i in devices]
    return lax.ppermute(block, axis, route)


def sum_in_order(pieces, axes, order):
    inside = pieces.shape[1:]
    pieces = pieces.reshape(*(lax.axis_size(a) for a in axes), *inside)
    pieces = jnp.moveaxis(pieces, order, range(len(axes))).reshape(-1, *inside)
    for k in order:
        pieces = lax.psum_scatter(pieces, axes[k], scatter_dimension=0, tiled=True)
    return pieces[0]


def in_blocks(value, dim, length):
    shape = value.shape
    pieces = value.reshape(*shape[:dim], length, shape[dim] // length, *shape[dim + 1 :])
    return jnp.moveaxis(pieces, dim, 0)


def sum_by_axis(value, axes, order, dim):
    length = lax.axis_size(axes)
    return sum_in_order(in_blocks(value, dim, length), axes, order)


def rotate(vectors, positions):
    half_size = vectors.shape[-1] // 2
    exponent = jnp.arange(half_size, dtype=jnp.float32) * (2.0 / vectors.shape[-1])
    inverse_freq = theta_base ** (-exponent)
    angles = positions.astype(jnp.float32)[:, None] * inverse_freq[None, :]
    cosine = jnp.cos(angles)[:, None, :]
    sine_part = jnp.sin(angles)[:, None, :]
    lower_half = vectors[..., :half_size]
    upper_half = vectors[..., half_size:]
    return jnp.concatenate(
        [
            lower_half * cosine - upper_half * sine_part,
            upper_half * cosine + lower_half * sine_part,
        ],
        axis=-1,
    )


def block_update(
    carried, block_queries, query_index, query_start, block_keys, block_values, key_index
):
    row_max, weight_sum, weighted = carried
    scale_factor = block_queries.shape[-1] ** (-0.5)
    scores = (
        jnp.einsum("hrd,kd->hrk", block_queries, block_keys, preferred_element_type=jnp.float32)
        * scale_factor
    )
    visible = (
        (key_index[None, :] <= query_index[:, None]) & (key_index[None, :] >= query_start[:, None])
    )[None]
    scores = jnp.where(visible, scores, floor_score)
    new_max = jnp.maximum(row_max, jnp.max(scores, axis=-1))
    weights = jnp.where(visible, jnp.exp(scores - new_max[..., None]), 0.0)
    rescale = jnp.exp(row_max - new_max)
    weight_sum = weight_sum * rescale + jnp.sum(weights, axis=-1)
    weighted = weighted * rescale[..., None] + jnp.einsum(
        "hrk,kd->hrd",
        weights.astype(jnp.bfloat16),
        block_values,
        preferred_element_type=jnp.float32,
    )
    return (new_max, weight_sum, weighted)


def keep_state(carried):
    return carried


def attend(halves, query_parts, key_block, value_block, key_index):
    half_rows = key_block.shape[0] // 2
    updated = []
    for query_half in range(2):
        carried = halves[query_half]
        block_queries, query_index, query_start = query_parts[query_half]
        lowest_start = jnp.min(query_start)
        for key_half in range(2):
            key_rows = lax.slice_in_dim(
                key_block, key_half * half_rows, (key_half + 1) * half_rows, axis=0
            )
            value_rows = lax.slice_in_dim(
                value_block, key_half * half_rows, (key_half + 1) * half_rows, axis=0
            )
            index_rows = lax.slice_in_dim(
                key_index, key_half * half_rows, (key_half + 1) * half_rows, axis=0
            )
            needed = (index_rows[0] <= query_index[-1]) & (index_rows[-1] >= lowest_start)
            update_fn = partial(
                block_update,
                block_queries=block_queries,
                query_index=query_index,
                query_start=query_start,
                block_keys=key_rows,
                block_values=value_rows,
                key_index=index_rows,
            )
            carried = lax.cond(needed, update_fn, keep_state, carried)
        updated.append(carried)
    return tuple(updated)


def per_device(tokens, span_ids, positions, q_weight, k_weight, v_weight, o_weight):
    row_count = tokens.shape[0]
    half_rows = row_count // 2
    head_count = q_weight.shape[1] // HD
    weights_in = (q_weight, k_weight, v_weight)
    pieces = lax.all_gather(tokens, TP, axis=1, tiled=True)
    queries, keys_here, values_here = tuple(
        (jnp.dot(pieces, matrix, preferred_element_type=jnp.float32) for matrix in weights_in)
    )
    queries = rotate(queries.reshape(row_count, head_count, HD), positions).astype(jnp.bfloat16)
    queries = jnp.transpose(queries, (1, 0, 2))
    keys_here = (
        rotate(keys_here.reshape(row_count, 1, HD), positions)
        .reshape(row_count, HD)
        .astype(jnp.bfloat16)
    )
    values_here = values_here.astype(jnp.bfloat16)
    span_table = gather_axes(span_ids, (("cp_0", "cp_1"), "cp_2"), (0, 1), 0)
    rank_count = span_table.shape[0]
    offsets = jnp.arange(half_rows, dtype=jnp.int32)
    global_index = (span_table[:, :, None] * half_rows + offsets[None, None, :]).reshape(
        rank_count * row_count
    )
    my_rank = lax.axis_index(CP)
    own_index = lax.dynamic_slice_in_dim(global_index, my_rank * row_count, row_count)
    doc_start = own_index - positions
    query_parts = tuple(
        (
            (
                queries[:, part_index * half_rows : (part_index + 1) * half_rows],
                own_index[part_index * half_rows : (part_index + 1) * half_rows],
                doc_start[part_index * half_rows : (part_index + 1) * half_rows],
            )
            for part_index in range(2)
        )
    )
    empty_state = (
        jnp.full((head_count, half_rows), floor_score, jnp.float32),
        jnp.zeros((head_count, half_rows), jnp.float32),
        jnp.zeros((head_count, half_rows, HD), jnp.float32),
    )
    halves = (empty_state, empty_state)
    halves = attend(halves, query_parts, keys_here, values_here, own_index)

    def turn(turn_index, loop_state):
        carried, moving = loop_state
        moving = from_behind(moving, CP, 1)
        source = (my_rank - turn_index - 1) % rank_count
        key_index = lax.dynamic_slice_in_dim(global_index, source * row_count, row_count)
        return (attend(carried, query_parts, moving[0], moving[1], key_index), moving)

    halves, moved_last = lax.fori_loop(
        0, rank_count - 1, turn, (halves, jnp.stack((keys_here, values_here)))
    )
    outputs = []
    for carried in halves:
        outputs.append(carried[2] / carried[1][..., None])
    attention = jnp.concatenate(outputs, axis=1).astype(jnp.bfloat16)
    out_weight = o_weight.reshape(head_count, HD, o_weight.shape[1])
    partial_sum = jnp.einsum(
        "hrd,hdn->rn", attention, out_weight, preferred_element_type=jnp.float32
    )
    return (
        sum_by_axis(partial_sum.astype(jnp.bfloat16), TP, (1, 0), 1)
        .astype(jnp.float32)
        .astype(jnp.bfloat16)
    )


def solution(mesh):
    split = Mesh(mesh.devices.reshape(4, 4, 2, 2, 4), ("cp_0", "cp_1", "cp_2", "tp_0", "tp_1"))
    placed = (P(CP, TP), P(CP, None), P(CP), P(None, TP), P(None, TP), P(None, TP), P(TP, None))
    return jax.shard_map(
        per_device, mesh=split, in_specs=placed, out_specs=P(CP, TP), check_vma=False
    )
```

profile of v0, /device:TPU:16, one launch (start us, length us, event | category | flops | bytes accessed | tf_op | source)
XLA Modules:
  0.0 776.8 jit_solution(6277096617553391568)
XLA Ops:
  7.3 39.4 %all-gather.2 = s32[16,1,2]{2,1,0:T(1,128)S(1)} all-gather(s32[1,1,2]{2,1,0:T(1,128)} %bitcast.155), channel_id=2, replica_groups=mesh['cp_0'=4,'cp_1'=4,'cp_2'=2,'tp_0'=2,'tp_1'=4] {'cp_0','cp_1'}, dimensions={0}, use_global_device_ids=true | all-gather | bytes 136 | tf_op jit(solution)/shard_map/all_gather | solution.py:27
  63.0 60.4 %all-gather.6.cloned.1.call-done = bf16[512,4096]{1,0:T(8,128)(2,1)} async-done(((bf16[512,512]{1,0:T(8,128)(2,1)}), bf16[512,4096]{1,0:T(8,128)(2,1)}) %all-gather.6.cloned.1.call-update) | async-done | bytes 4194320 | tf_op jit(solution)/shard_map/all_gather | solution.py:149
  123.4 3.8 convolution_bitcast_fusion
  137.9 3.8 conditional.8
  142.4 3.2 conditional.11
  145.6 502.3 %while.27 = (s32[]{:T(128)}, f32[4,256]{1,0:T(4,128)}, f32[4,256]{1,0:T(4,128)S(1)}, f32[4,256,128]{2,1,0:T(8,128)S(1)}, f32[4,256]{1,0:T(4,128)}, /*index=5*/f3...) while((s32[]{:T(128)}, f32[4,256]{1,0:T(4,128)}, ...), condition=%wide.region_35.36_spmd, body=%wide.region_18.35_spmd.sunk | while | flops 548151296 | bytes 21779492 | solution.py:195
  207.5 3.2 conditional.16
  239.5 3.2 conditional.17
  272.9 3.2 conditional.17
  306.5 3.2 conditional.16
  322.4 3.2 conditional.16
  388.4 4.6 collective-permute-start
  405.0 3.2 conditional.16
  437.0 3.2 conditional.16
  500.9 3.2 conditional.17
  564.7 3.2 conditional.16
  599.1 3.2 conditional.16
  615.0 3.2 conditional.16
  648.2 5.1 bitcast_convert_fusion
  653.3 4.2 copy.110
  657.5 6.9 reshape.630
  664.4 5.5 copy.79
  670.0 56.9 %reduce-scatter.3.cloned.1.call-done = bf16[2,512,512]{2,1,0:T(8,128)(2,1)} async-done(((bf16[8,512,512]{2,1,0:T(8,128)(2,1)}), bf16[2,512,512]{2,1,0:T(8,128)(2,1)}) %reduce-scatter.3.cloned.1.call-update) | async-done | bytes 1048592 | tf_op jit(solution)/shard_map/reduce_scatter | solution.py:49
  727.0 43.3 %reduce-scatter.5.cloned.1.call-done = bf16[1,512,512]{2,1,0:T(8,128)(2,1)} async-done(((bf16[2,512,512]{2,1,0:T(8,128)(2,1)}), bf16[1,512,512]{2,1,0:T(8,128)(2,1)}) %reduce-scatter.5.cloned.1.call-update) | async-done | bytes 524304 | tf_op jit(solution)/shard_map/reduce_scatter | solution.py:49
  (605 shorter events, 246.7 us)
Async XLA Ops:
  6.5 116.8 %all-gather.6.cloned.1.call-start = ((), (), s32[]{:S(2)}) async-start(), calls=%async_computation.2 | async-start | bytes 4718592 | tf_op jit(solution)/shard_map/all_gather | solution.py:149
  7.3 719.7 %reduce-scatter.3.cloned.1.call-start = ((), (), s32[]{:S(2)}) async-start(), calls=%async_computation.3 | async-start | bytes 5242880 | tf_op jit(solution)/shard_map/reduce_scatter | solution.py:49
  161.5 13.3 %collective-permute-start = (bf16[2,512,128]{2,1,0:T(8,128)(2,1)}, bf16[2,512,128]{2,1,0:T(8,128)(2,1)S(1)}, u32[]{:S(2)}, u32[]{:S(2)}) collective-permute-start(bf16[2,512,128]{2,1,0:T(8,128)(2,1)} %get-tuple-element.1174), channel_id=1, source_target_pairs={{248,0},{0,8},{8,16},{16,24},{24,32},{32,40},{40,48},{48,56},{56,6... | collective-permute-start | bytes 786440 | tf_op jit(solution)/shard_map/while/body/eval_jaxpr/ppermute | solution.py:41
  175.7 15.1 %collective-permute-start = (bf16[2,512,128]{2,1,0:T(8,128)(2,1)}, bf16[2,512,128]{2,1,0:T(8,128)(2,1)S(1)}, u32[]{:S(2)}, u32[]{:S(2)}) collective-permute-start(bf16[2,512,128]{2,1,0:T(8,128)(2,1)} %get-tuple-element.1174), channel_id=1, source_target_pairs={{248,0},{0,8},{8,16},{16,24},{24,32},{32,40},{40,48},{48,56},{56,6... | collective-permute-start | bytes 786440 | tf_op jit(solution)/shard_map/while/body/eval_jaxpr/ppermute | solution.py:41
  194.8 12.7 %collective-permute-start = (bf16[2,512,128]{2,1,0:T(8,128)(2,1)}, bf16[2,512,128]{2,1,0:T(8,128)(2,1)S(1)}, u32[]{:S(2)}, u32[]{:S(2)}) collective-permute-start(bf16[2,512,128]{2,1,0:T(8,128)(2,1)} %get-tuple-element.1174), channel_id=1, source_target_pairs={{248,0},{0,8},{8,16},{16,24},{24,32},{32,40},{40,48},{48,56},{56,6... | collective-permute-start | bytes 786440 | tf_op jit(solution)/shard_map/while/body/eval_jaxpr/ppermute | solution.py:41
  227.4 12.0 %collective-permute-start = (bf16[2,512,128]{2,1,0:T(8,128)(2,1)}, bf16[2,512,128]{2,1,0:T(8,128)(2,1)S(1)}, u32[]{:S(2)}, u32[]{:S(2)}) collective-permute-start(bf16[2,512,128]{2,1,0:T(8,128)(2,1)} %get-tuple-element.1174), channel_id=1, source_target_pairs={{248,0},{0,8},{8,16},{16,24},{24,32},{32,40},{40,48},{48,56},{56,6... | collective-permute-start | bytes 786440 | tf_op jit(solution)/shard_map/while/body/eval_jaxpr/ppermute | solution.py:41
  243.4 13.5 %collective-permute-start = (bf16[2,512,128]{2,1,0:T(8,128)(2,1)}, bf16[2,512,128]{2,1,0:T(8,128)(2,1)S(1)}, u32[]{:S(2)}, u32[]{:S(2)}) collective-permute-start(bf16[2,512,128]{2,1,0:T(8,128)(2,1)} %get-tuple-element.1174), channel_id=1, source_target_pairs={{248,0},{0,8},{8,16},{16,24},{24,32},{32,40},{40,48},{48,56},{56,6... | collective-permute-start | bytes 786440 | tf_op jit(solution)/shard_map/while/body/eval_jaxpr/ppermute | solution.py:41
  257.8 15.1 %collective-permute-start = (bf16[2,512,128]{2,1,0:T(8,128)(2,1)}, bf16[2,512,128]{2,1,0:T(8,128)(2,1)S(1)}, u32[]{:S(2)}, u32[]{:S(2)}) collective-permute-start(bf16[2,512,128]{2,1,0:T(8,128)(2,1)} %get-tuple-element.1174), channel_id=1, source_target_pairs={{248,0},{0,8},{8,16},{16,24},{24,32},{32,40},{40,48},{48,56},{56,6... | collective-permute-start | bytes 786440 | tf_op jit(solution)/shard_map/while/body/eval_jaxpr/ppermute | solution.py:41
  276.8 13.6 %collective-permute-start = (bf16[2,512,128]{2,1,0:T(8,128)(2,1)}, bf16[2,512,128]{2,1,0:T(8,128)(2,1)S(1)}, u32[]{:S(2)}, u32[]{:S(2)}) collective-permute-start(bf16[2,512,128]{2,1,0:T(8,128)(2,1)} %get-tuple-element.1174), channel_id=1, source_target_pairs={{248,0},{0,8},{8,16},{16,24},{24,32},{32,40},{40,48},{48,56},{56,6... | collective-permute-start | bytes 786440 | tf_op jit(solution)/shard_map/while/body/eval_jaxpr/ppermute | solution.py:41
  291.3 15.1 %collective-permute-start = (bf16[2,512,128]{2,1,0:T(8,128)(2,1)}, bf16[2,512,128]{2,1,0:T(8,128)(2,1)S(1)}, u32[]{:S(2)}, u32[]{:S(2)}) collective-permute-start(bf16[2,512,128]{2,1,0:T(8,128)(2,1)} %get-tuple-element.1174), channel_id=1, source_target_pairs={{248,0},{0,8},{8,16},{16,24},{24,32},{32,40},{40,48},{48,56},{56,6... | collective-permute-start | bytes 786440 | tf_op jit(solution)/shard_map/while/body/eval_jaxpr/ppermute | solution.py:41
  326.3 13.4 %collective-permute-start = (bf16[2,512,128]{2,1,0:T(8,128)(2,1)}, bf16[2,512,128]{2,1,0:T(8,128)(2,1)S(1)}, u32[]{:S(2)}, u32[]{:S(2)}) collective-permute-start(bf16[2,512,128]{2,1,0:T(8,128)(2,1)} %get-tuple-element.1174), channel_id=1, source_target_pairs={{248,0},{0,8},{8,16},{16,24},{24,32},{32,40},{40,48},{48,56},{56,6... | collective-permute-start | bytes 786440 | tf_op jit(solution)/shard_map/while/body/eval_jaxpr/ppermute | solution.py:41
  343.6 12.0 %collective-permute-start = (bf16[2,512,128]{2,1,0:T(8,128)(2,1)}, bf16[2,512,128]{2,1,0:T(8,128)(2,1)S(1)}, u32[]{:S(2)}, u32[]{:S(2)}) collective-permute-start(bf16[2,512,128]{2,1,0:T(8,128)(2,1)} %get-tuple-element.1174), channel_id=1, source_target_pairs={{248,0},{0,8},{8,16},{16,24},{24,32},{32,40},{40,48},{48,56},{56,6... | collective-permute-start | bytes 786440 | tf_op jit(solution)/shard_map/while/body/eval_jaxpr/ppermute | solution.py:41
  356.5 15.1 %collective-permute-start = (bf16[2,512,128]{2,1,0:T(8,128)(2,1)}, bf16[2,512,128]{2,1,0:T(8,128)(2,1)S(1)}, u32[]{:S(2)}, u32[]{:S(2)}) collective-permute-start(bf16[2,512,128]{2,1,0:T(8,128)(2,1)} %get-tuple-element.1174), channel_id=1, source_target_pairs={{248,0},{0,8},{8,16},{16,24},{24,32},{32,40},{40,48},{48,56},{56,6... | collective-permute-start | bytes 786440 | tf_op jit(solution)/shard_map/while/body/eval_jaxpr/ppermute | solution.py:41
  388.4 16.6 %collective-permute-start = (bf16[2,512,128]{2,1,0:T(8,128)(2,1)}, bf16[2,512,128]{2,1,0:T(8,128)(2,1)S(1)}, u32[]{:S(2)}, u32[]{:S(2)}) collective-permute-start(bf16[2,512,128]{2,1,0:T(8,128)(2,1)} %get-tuple-element.1174), channel_id=1, source_target_pairs={{248,0},{0,8},{8,16},{16,24},{24,32},{32,40},{40,48},{48,56},{56,6... | collective-permute-start | bytes 786440 | tf_op jit(solution)/shard_map/while/body/eval_jaxpr/ppermute | solution.py:41
  408.9 12.1 %collective-permute-start = (bf16[2,512,128]{2,1,0:T(8,128)(2,1)}, bf16[2,512,128]{2,1,0:T(8,128)(2,1)S(1)}, u32[]{:S(2)}, u32[]{:S(2)}) collective-permute-start(bf16[2,512,128]{2,1,0:T(8,128)(2,1)} %get-tuple-element.1174), channel_id=1, source_target_pairs={{248,0},{0,8},{8,16},{16,24},{24,32},{32,40},{40,48},{48,56},{56,6... | collective-permute-start | bytes 786440 | tf_op jit(solution)/shard_map/while/body/eval_jaxpr/ppermute | solution.py:41
  424.9 12.0 %collective-permute-start = (bf16[2,512,128]{2,1,0:T(8,128)(2,1)}, bf16[2,512,128]{2,1,0:T(8,128)(2,1)S(1)}, u32[]{:S(2)}, u32[]{:S(2)}) collective-permute-start(bf16[2,512,128]{2,1,0:T(8,128)(2,1)} %get-tuple-element.1174), channel_id=1, source_target_pairs={{248,0},{0,8},{8,16},{16,24},{24,32},{32,40},{40,48},{48,56},{56,6... | collective-permute-start | bytes 786440 | tf_op jit(solution)/shard_map/while/body/eval_jaxpr/ppermute | solution.py:41
  453.8 15.1 %collective-permute-start = (bf16[2,512,128]{2,1,0:T(8,128)(2,1)}, bf16[2,512,128]{2,1,0:T(8,128)(2,1)S(1)}, u32[]{:S(2)}, u32[]{:S(2)}) collective-permute-start(bf16[2,512,128]{2,1,0:T(8,128)(2,1)} %get-tuple-element.1174), channel_id=1, source_target_pairs={{248,0},{0,8},{8,16},{16,24},{24,32},{32,40},{40,48},{48,56},{56,6... | collective-permute-start | bytes 786440 | tf_op jit(solution)/shard_map/while/body/eval_jaxpr/ppermute | solution.py:41
  469.7 15.1 %collective-permute-start = (bf16[2,512,128]{2,1,0:T(8,128)(2,1)}, bf16[2,512,128]{2,1,0:T(8,128)(2,1)S(1)}, u32[]{:S(2)}, u32[]{:S(2)}) collective-permute-start(bf16[2,512,128]{2,1,0:T(8,128)(2,1)} %get-tuple-element.1174), channel_id=1, source_target_pairs={{248,0},{0,8},{8,16},{16,24},{24,32},{32,40},{40,48},{48,56},{56,6... | collective-permute-start | bytes 786440 | tf_op jit(solution)/shard_map/while/body/eval_jaxpr/ppermute | solution.py:41
  485.7 15.1 %collective-permute-start = (bf16[2,512,128]{2,1,0:T(8,128)(2,1)}, bf16[2,512,128]{2,1,0:T(8,128)(2,1)S(1)}, u32[]{:S(2)}, u32[]{:S(2)}) collective-permute-start(bf16[2,512,128]{2,1,0:T(8,128)(2,1)} %get-tuple-element.1174), channel_id=1, source_target_pairs={{248,0},{0,8},{8,16},{16,24},{24,32},{32,40},{40,48},{48,56},{56,6... | collective-permute-start | bytes 786440 | tf_op jit(solution)/shard_map/while/body/eval_jaxpr/ppermute | solution.py:41
  584.5 14.5 %collective-permute-start = (bf16[2,512,128]{2,1,0:T(8,128)(2,1)}, bf16[2,512,128]{2,1,0:T(8,128)(2,1)S(1)}, u32[]{:S(2)}, u32[]{:S(2)}) collective-permute-start(bf16[2,512,128]{2,1,0:T(8,128)(2,1)} %get-tuple-element.1174), channel_id=1, source_target_pairs={{248,0},{0,8},{8,16},{16,24},{24,32},{32,40},{40,48},{48,56},{56,6... | collective-permute-start | bytes 786440 | tf_op jit(solution)/shard_map/while/body/eval_jaxpr/ppermute | solution.py:41
  602.9 12.1 %collective-permute-start = (bf16[2,512,128]{2,1,0:T(8,128)(2,1)}, bf16[2,512,128]{2,1,0:T(8,128)(2,1)S(1)}, u32[]{:S(2)}, u32[]{:S(2)}) collective-permute-start(bf16[2,512,128]{2,1,0:T(8,128)(2,1)} %get-tuple-element.1174), channel_id=1, source_target_pairs={{248,0},{0,8},{8,16},{16,24},{24,32},{32,40},{40,48},{48,56},{56,6... | collective-permute-start | bytes 786440 | tf_op jit(solution)/shard_map/while/body/eval_jaxpr/ppermute | solution.py:41
  618.9 12.1 %collective-permute-start = (bf16[2,512,128]{2,1,0:T(8,128)(2,1)}, bf16[2,512,128]{2,1,0:T(8,128)(2,1)S(1)}, u32[]{:S(2)}, u32[]{:S(2)}) collective-permute-start(bf16[2,512,128]{2,1,0:T(8,128)(2,1)} %get-tuple-element.1174), channel_id=1, source_target_pairs={{248,0},{0,8},{8,16},{16,24},{24,32},{32,40},{40,48},{48,56},{56,6... | collective-permute-start | bytes 786440 | tf_op jit(solution)/shard_map/while/body/eval_jaxpr/ppermute | solution.py:41
  635.0 12.0 %collective-permute-start = (bf16[2,512,128]{2,1,0:T(8,128)(2,1)}, bf16[2,512,128]{2,1,0:T(8,128)(2,1)S(1)}, u32[]{:S(2)}, u32[]{:S(2)}) collective-permute-start(bf16[2,512,128]{2,1,0:T(8,128)(2,1)} %get-tuple-element.1174), channel_id=1, source_target_pairs={{248,0},{0,8},{8,16},{16,24},{24,32},{32,40},{40,48},{48,56},{56,6... | collective-permute-start | bytes 786440 | tf_op jit(solution)/shard_map/while/body/eval_jaxpr/ppermute | solution.py:41
  670.0 100.3 %reduce-scatter.5.cloned.1.call-start = ((), (), s32[]{:S(2)}) async-start(), calls=%async_computation.4 | async-start | bytes 1572864 | tf_op jit(solution)/shard_map/reduce_scatter | solution.py:49
  (14 other events, 309.9 us)
Sparse Core Ops, SparseCore 0:
  9.8 113.4 all-gather.5
  670.1 56.8 reduce-scatter.2
  729.5 40.7 reduce-scatter.4
where the time goes:
time: 780 us; the launch traced here: 777 us
  loops' own time  313 us (40%)
  waiting for transfers between devices  161 us (21%)
  local copies, waits for them, and re-layouts  119 us (15%)
  other arithmetic  48.8 us (6%)
  blocking collectives  41.2 us (5%)
  starting transfers between devices  36 us (5%)
  matrix products  33.4 us (4%)
  between operations  23.4 us (3%)
    another operation x1, loops' own time, per_device(): lax.fori_loop(0, rank_count - 1, turn, (halves, jnp.stack((keys_here, val...  311 us
    reduce_scatter x2, waiting for transfers between devices, sum_in_order(): pieces = lax.psum_scatter(pieces, axes[k], scatter_dimension=0, tiled=True)  100 us
    all_gather x1, waiting for transfers between devices, per_device(): pieces = lax.all_gather(tokens, TP, axis=1, tiled=True)  60.4 us
    all_gather x2, blocking collectives, all_blocks(): pieces = lax.all_gather(pieces, axes[k], axis=0, tiled=True)  41.2 us
    slice x62, local copies, waits for them, and re-layouts, attend(): query_index[-1]  38.8 us
    ppermute x31, starting transfers between devices, from_behind(): return lax.ppermute(block, axis, route)  35.9 us
    while x31, local copies, waits for them, and re-layouts  21.6 us
    slice x31, local copies, waits for them, and re-layouts, attend(): index_rows[-1] >= lowest_start  20.7 us
  transfers between devices with their start and end apart: 34, of which 3 were waited for; matrix products, arithmetic and copies ran while one was open for 9% of the time, Pallas kernels for 0%

commit v1 on v0

v1 whole, which is shorter than its diff:
```python
import jax
import jax.numpy as jnp
from jax import lax
from jax.experimental import pallas as pl
from jax.experimental.pallas import tpu as pltpu
from jax.sharding import Mesh
from jax.sharding import PartitionSpec as P

HD = 128
TP = ("tp_0", "tp_1")
CP = ("cp_0", "cp_1", "cp_2")


theta_base = 500000.0
floor_score = -1e30


def sum_in_order(pieces, axes, order):
    inside = pieces.shape[1:]
    pieces = pieces.reshape(*(lax.axis_size(a) for a in axes), *inside)
    pieces = jnp.moveaxis(pieces, order, range(len(axes))).reshape(-1, *inside)
    for k in order:
        pieces = lax.psum_scatter(pieces, axes[k], scatter_dimension=0, tiled=True)
    return pieces[0]


def in_blocks(value, dim, length):
    shape = value.shape
    pieces = value.reshape(*shape[:dim], length, shape[dim] // length, *shape[dim + 1 :])
    return jnp.moveaxis(pieces, dim, 0)


def sum_by_axis(value, axes, order, dim):
    length = lax.axis_size(axes)
    return sum_in_order(in_blocks(value, dim, length), axes, order)


def rotate(vectors, positions):
    half_size = vectors.shape[-1] // 2
    exponent = jnp.arange(half_size, dtype=jnp.float32) * (2.0 / vectors.shape[-1])
    inverse_freq = theta_base ** (-exponent)
    angles = positions.astype(jnp.float32)[:, None] * inverse_freq[None, :]
    cosine = jnp.cos(angles)[:, None, :]
    sine_part = jnp.sin(angles)[:, None, :]
    lower_half = vectors[..., :half_size]
    upper_half = vectors[..., half_size:]
    return jnp.concatenate(
        [
            lower_half * cosine - upper_half * sine_part,
            upper_half * cosine + lower_half * sine_part,
        ],
        axis=-1,
    )


SPAN = 256
LOG2E = 1.4426950408889634


def attend_kernel(info, q_ref, kv_ref, start_ref, out_ref, top_ref, acc_ref):
    heads = q_ref.shape[1] // SPAN
    scale = LOG2E * HD**-0.5
    ones = jnp.ones((SPAN, HD), jnp.bfloat16)

    def block(half, span, masked, first):
        place = info[span]
        rank, part = place // 2, place % 2
        keys = kv_ref[rank, pl.ds(pl.multiple_of(part * SPAN, SPAN), SPAN), :]
        values = kv_ref[rank, pl.ds(pl.multiple_of((2 + part) * SPAN, SPAN), SPAN), :]
        values = jnp.concatenate([values, ones], axis=1)
        if masked:
            key = span * SPAN + lax.broadcasted_iota(jnp.int32, (SPAN, SPAN), 1)
            start = start_ref[half]
            seen = key >= jnp.concatenate([start, start], axis=1)
            if first:
                query = span * SPAN + lax.broadcasted_iota(jnp.int32, (SPAN, SPAN), 0)
                seen = seen & (key <= query)
        for head in range(heads):
            rows = slice(head * SPAN, (head + 1) * SPAN)
            score = lax.dot_general(
                q_ref[half, rows, :],
                keys,
                (((1,), (1,)), ((), ())),
                preferred_element_type=jnp.float32,
            )
            score = score * scale
            if masked:
                score = jnp.where(seen, score, floor_score)
            top = jnp.max(score, axis=1, keepdims=True)
            if first:
                weight = jnp.exp2(score - top)
                top_ref[rows, :] = jnp.broadcast_to(top, (SPAN, HD))
            else:
                before = top_ref[rows, :]
                now = jnp.maximum(before, top)
                weight = jnp.exp2(score - jnp.concatenate([now, now], axis=1))
                fade = jnp.exp2(before - now)
                top_ref[rows, :] = now
            mixed = jnp.dot(
                weight.astype(jnp.bfloat16), values, preferred_element_type=jnp.float32
            )
            if not first:
                mixed = mixed + acc_ref[rows, :] * jnp.concatenate([fade, fade], axis=1)
            acc_ref[rows, :] = mixed

    for half in range(2):
        own, low, clear = info[64 + half], info[66 + half], info[68 + half]
        block(half, own, True, True)
        lax.fori_loop(low, clear, lambda s, c: (block(half, s, True, False), c)[1], 0)
        lax.fori_loop(clear, own, lambda s, c: (block(half, s, False, False), c)[1], 0)
        for head in range(heads):
            rows = slice(head * SPAN, (head + 1) * SPAN)
            mixed = acc_ref[rows, :HD] / acc_ref[rows, HD:]
            out_ref[half * SPAN : (half + 1) * SPAN, head * HD : (head + 1) * HD] = mixed.astype(
                jnp.bfloat16
            )


def attend(info, queries, gathered, starts):
    vmem = pl.BlockSpec(memory_space=pltpu.VMEM)
    rows = queries.shape[1]
    heads = rows // SPAN
    return pl.pallas_call(
        attend_kernel,
        out_shape=jax.ShapeDtypeStruct((2 * SPAN, heads * HD), jnp.bfloat16),
        in_specs=[pl.BlockSpec(memory_space=pltpu.SMEM), vmem, vmem, vmem],
        out_specs=vmem,
        scratch_shapes=[
            pltpu.VMEM((rows, HD), jnp.float32),
            pltpu.VMEM((rows, 2 * HD), jnp.float32),
        ],
        compiler_params=pltpu.CompilerParams(vmem_limit_bytes=32 * 1024 * 1024),
        name="attend",
    )(info, queries, gathered, starts)


def plan(span_table, own, starts):
    blocks = jnp.arange(64, dtype=jnp.int32)
    where = jnp.sum(
        jnp.where(span_table.reshape(1, 64) == blocks[:, None], blocks[None, :], 0), axis=1
    )
    low = starts[:, 0] // SPAN
    clear = jnp.minimum((starts[:, -1] + SPAN - 1) // SPAN, own)
    return jnp.concatenate([where, own, low, clear, jnp.zeros(58, jnp.int32)])


def per_device(tokens, span_ids, positions, q_weight, k_weight, v_weight, o_weight):
    row_count = tokens.shape[0]
    half_rows = row_count // 2
    head_count = q_weight.shape[1] // HD
    weights_in = (q_weight, k_weight, v_weight)
    pieces = lax.all_gather(tokens, TP, axis=1, tiled=True)
    queries, keys_here, values_here = tuple(
        (jnp.dot(pieces, matrix, preferred_element_type=jnp.float32) for matrix in weights_in)
    )
    queries = rotate(queries.reshape(row_count, head_count, HD), positions).astype(jnp.bfloat16)
    queries = jnp.transpose(queries, (1, 0, 2))
    keys_here = (
        rotate(keys_here.reshape(row_count, 1, HD), positions)
        .reshape(row_count, HD)
        .astype(jnp.bfloat16)
    )
    values_here = values_here.astype(jnp.bfloat16)
    own = span_ids.reshape(2)
    own_rows = jnp.repeat(own.astype(jnp.bfloat16), 8)[:, None] * jnp.ones((1, HD), jnp.bfloat16)
    held = jnp.concatenate([keys_here, values_here, own_rows], axis=0)
    gathered = lax.all_gather(held, CP, axis=0, tiled=False)
    span_table = gathered[:, 2 * row_count :: 8, 0].astype(jnp.int32)
    offsets = jnp.arange(half_rows, dtype=jnp.int32)
    starts = own[:, None] * half_rows + offsets[None, :] - positions.reshape(2, half_rows)
    info = plan(span_table, own, starts)
    starts = jnp.broadcast_to(starts[:, :, None], (2, half_rows, HD))
    queries = queries.reshape(head_count, 2, half_rows, HD).transpose(1, 0, 2, 3)
    attention = attend(info, queries.reshape(2, head_count * half_rows, HD), gathered, starts)
    attention = attention.reshape(row_count, head_count, HD)
    out_weight = o_weight.reshape(head_count, HD, o_weight.shape[1])
    partial_sum = jnp.einsum(
        "rhd,hdn->rn", attention, out_weight, preferred_element_type=jnp.float32
    )
    return (
        sum_by_axis(partial_sum.astype(jnp.bfloat16), TP, (1, 0), 1)
        .astype(jnp.float32)
        .astype(jnp.bfloat16)
    )


def solution(mesh):
    split = Mesh(mesh.devices.reshape(4, 4, 2, 2, 4), ("cp_0", "cp_1", "cp_2", "tp_0", "tp_1"))
    placed = (P(CP, TP), P(CP, None), P(CP), P(None, TP), P(None, TP), P(None, TP), P(TP, None))
    return jax.shard_map(
        per_device, mesh=split, in_specs=placed, out_specs=P(CP, TP), check_vma=False
    )
```

time: 780 us -> 341 us (0.44)
  loops' own time: 313 us -> 0 us
  waiting for transfers between devices: 161 us -> 262 us
  local copies, waits for them, and re-layouts: 119 us -> 25.1 us
  other arithmetic: 48.8 us -> 6.36 us
  blocking collectives: 41.2 us -> 0 us
  starting transfers between devices: 36 us -> 0.12 us
  matrix products: 33.4 us -> 13.7 us
  Pallas kernels: 0 us -> 18.8 us
  between operations: 23.4 us -> 13.3 us
    another operation x129 -> x0, loops' own time: 313 us -> none  [the longest x1 311 us: per_device(): lax.fori_loop(0, rank_count - 1, turn, (halves, jnp.stack((keys_here, val...]
    slice x160 -> x1, local copies, waits for them, and re-layouts: 61.9 us -> 0.94 us  [per_device(): span_table = gathered[:, 2 * row_count::8, 0].astype(jnp.int32)]
    all_gather x1, waiting for transfers between devices: 60.4 us -> 114 us  [per_device(): pieces = lax.all_gather(tokens, TP, axis=1, tiled=True)]
    all_gather x0 -> x1, waiting for transfers between devices: none -> 51.7 us  [per_device(): gathered = lax.all_gather(held, CP, axis=0, tiled=False)]
    all_gather x2 -> x0, blocking collectives: 41.2 us -> none  [all_blocks(): pieces = lax.all_gather(pieces, axes[k], axis=0, tiled=True)]
    ppermute x31 -> x0, starting transfers between devices: 35.9 us -> none  [from_behind(): return lax.ppermute(block, axis, route)]
    dot_general x49 -> x1, matrix products: 25.7 us -> 2.56 us  [per_device(): jnp.einsum('rhd,hdn->rn', attention, out_weight, preferred_element_type=j...]
    while x32 -> x0, local copies, waits for them, and re-layouts: 22.4 us -> none
  transfers between devices with their start and end apart: 34 -> 4, of which waited for: 3 -> 4; matrix products, arithmetic and copies ran while one was open for 9% -> 4% of each run, Pallas kernels for 0% -> 0%
where the time goes in v1:
time: 341 us; the launch traced here: 339 us
  waiting for transfers between devices  262 us (77%)
  local copies, waits for them, and re-layouts  25.1 us (7%)
  Pallas kernels  18.8 us (6%)
  matrix products  13.7 us (4%)
  between operations  13.3 us (4%)
  other arithmetic  6.36 us (2%)
    all_gather x1, waiting for transfers between devices, per_device(): pieces = lax.all_gather(tokens, TP, axis=1, tiled=True)  114 us
    reduce_scatter x2, waiting for transfers between devices, sum_in_order(): pieces = lax.psum_scatter(pieces, axes[k], scatter_dimension=0, tiled=True)  94.8 us
    all_gather x1, waiting for transfers between devices, per_device(): gathered = lax.all_gather(held, CP, axis=0, tiled=False)  51.7 us
    pallas_call x1, Pallas kernels, attend(): pl.pallas_call(attend_kernel, out_shape=jax.ShapeDtypeStruct((2 * SPAN, h...  18.8 us
    reshape x2, local copies, waits for them, and re-layouts, sum_in_order(): pieces = pieces.reshape(*(lax.axis_size(a) for a in axes), *inside)  12.5 us
    dot_general x3, matrix products, per_device(): jnp.dot(pieces, matrix, preferred_element_type=jnp.float32)  11.2 us
    unnamed x17, local copies, waits for them, and re-layouts  9.37 us
  transfers between devices with their start and end apart: 4, of which 4 were waited for; matrix products, arithmetic and copies ran while one was open for 4% of the time, Pallas kernels for 0%

profile of v1, /device:TPU:16, one launch (start us, length us, event | category | flops | bytes accessed | tf_op | source)
XLA Modules:
  0.0 339.1 jit_solution(9632764164141867831)
XLA Ops:
  6.5 0.7 all-gather.4.cloned.1.call-update
  7.3 0.8 convert_element_type.30
  8.1 0.7 bitcast_convert_fusion.1
  8.9 114.4 %all-gather.4.cloned.1.call-done = bf16[512,4096]{1,0:T(8,128)(2,1)} async-done(((bf16[512,512]{1,0:T(8,128)(2,1)}), bf16[512,4096]{1,0:T(8,128)(2,1)}) %all-gather.4.cloned.1.call-update) | async-done | bytes 4194320 | tf_op jit(solution)/shard_map/all_gather | solution.py:152
  123.3 3.8 %convolution_bitcast_fusion = f32[512,1,128]{0,2,1:T(8,128)S(1)} fusion(bf16[512,4096]{1,0:T(8,128)(2,1)} %all-gather.4.cloned.1.call-done, bf16[4096,128]{1,0:T(8,128)(2,1)S(1)} %copy-done), kind=kOutput, calls=%fused_computation.1 | convolution fusion | flops 536870912 | bytes 5505024 | tf_op jit(solution)/shard_map/dot_general | solution.py:154
  127.2 0.6 fusion.7
  127.8 1.5 convolution_convert_fusion
  129.4 0.9 copy.35
  130.7 1.8 multiply_cosine_fusion
  132.4 5.8 %fusion.13 = f32[512,512]{0,1:T(8,128)S(1)} fusion(bf16[512,4096]{1,0:T(8,128)(2,1)} %all-gather.4.cloned.1.call-done, bf16[4096,512]{1,0:T(8,128)(2,1)} %param.10), kind=kOutput, calls=%fused_computation.42 | convolution fusion | flops 2147483648 | bytes 9437184 | tf_op jit(solution)/shard_map/dot_general | solution.py:154
  138.3 0.9 fusion.12
  139.5 1.4 copy.43
  140.9 1.2 subtract_convert_fusion
  142.5 51.7 %all-gather.6.cloned.1.call-done = bf16[33280,128]{1,0:T(8,128)(2,1)} async-done(((bf16[1040,128]{1,0:T(8,128)(2,1)}), bf16[33280,128]{1,0:T(8,128)(2,1)}) %all-gather.6.cloned.1.call-update) | async-done | bytes 8519696 | tf_op jit(solution)/shard_map/all_gather | solution.py:167
  194.2 0.9 slice.23
  195.1 0.6 convert_reduce_fusion
  196.2 3.4 %copy-done.1 = bf16[33280,128]{1,0:T(8,128)(2,1)S(1)} copy-done((bf16[33280,128]{1,0:T(8,128)(2,1)S(1)}, bf16[33280,128]{1,0:T(8,128)(2,1)}, u32[]{:S(2)}) %copy-start.1) | copy-done | bytes 8519704
  199.6 18.8 %attend.1 = bf16[512,512]{1,0:T(8,128)(2,1)S(1)} custom-call(s32[128]{0:T(128)S(1)} %concatenate.16.info, bf16[2,1024,128]{2,1,0:T(8,128)(2,1)S(1)} %bitcast.45, bf16[32,1040,128]{2,1,0:T(8,128)(2,1)S(1)} %bitcast.44, s32[2,256,128]{2,1,0:T(8,128)S(1)} %broadcast_in_dim.22.start_ref), custom_call_target="tpu_custom_call" | custom-call | tf_op jit(solution)/shard_map/attend/pallas_call | solution.py:123
  218.4 2.6 bitcast_convert_fusion
  221.0 4.2 %copy.45 = bf16[64,8,8,512]{3,2,1,0:T(8,128)(2,1)} copy(bf16[64,8,8,512]{3,1,2,0:T(8,128)(2,1)S(1)} %bitcast.48) | data formatting | bytes 8388608
  225.2 6.9 %reshape.184 = bf16[2,4,512,512]{3,1,0,2:T(4,128)(2,1)} reshape(bf16[8,512,512]{2,0,1:T(8,128)(2,1)} %bitcast.47) | data formatting | bytes 8388608 | tf_op jit(solution)/shard_map/reshape | solution.py:20
  232.1 5.6 %copy.40 = bf16[2,4,512,512]{3,2,0,1:T(8,128)(2,1)} copy(bf16[2,4,512,512]{3,1,0,2:T(4,128)(2,1)} %reshape.184) | data formatting | bytes 8388608 | tf_op jit(solution)/shard_map/reshape | solution.py:20
  237.8 51.6 %reduce-scatter.3.cloned.1.call-done = bf16[2,512,512]{2,1,0:T(8,128)(2,1)} async-done(((bf16[8,512,512]{2,1,0:T(8,128)(2,1)}), bf16[2,512,512]{2,1,0:T(8,128)(2,1)}) %reduce-scatter.3.cloned.1.call-update) | async-done | bytes 1048592 | tf_op jit(solution)/shard_map/reduce_scatter | solution.py:23
  289.4 43.2 %reduce-scatter.5.cloned.1.call-done = bf16[1,512,512]{2,1,0:T(8,128)(2,1)} async-done(((bf16[2,512,512]{2,1,0:T(8,128)(2,1)}), bf16[1,512,512]{2,1,0:T(8,128)(2,1)}) %reduce-scatter.5.cloned.1.call-update) | async-done | bytes 524304 | tf_op jit(solution)/shard_map/reduce_scatter | solution.py:23
  (39 shorter events, 1.8 us)
Async XLA Ops:
  6.5 116.8 %copy-start = (bf16[4096,128]{1,0:T(8,128)(2,1)S(1)}, bf16[4096,128]{1,0:T(8,128)(2,1)}, u32[]{:S(2)}) copy-start(bf16[4096,128]{1,0:T(8,128)(2,1)} %param.11) | copy-start | bytes 3145732
  6.5 116.8 %all-gather.4.cloned.1.call-start = ((), (), s32[]{:S(2)}) async-start(), calls=%async_computation.2 | async-start | bytes 4718592 | tf_op jit(solution)/shard_map/all_gather | solution.py:152
  7.3 120.5 %copy-start.3 = (bf16[4096,128]{1,0:T(8,128)(2,1)S(1)}, bf16[4096,128]{1,0:T(8,128)(2,1)}, u32[]{:S(2)}) copy-start(bf16[4096,128]{1,0:T(8,128)(2,1)} %param.12) | copy-start | bytes 3145732
  7.3 186.9 %all-gather.6.cloned.1.call-start = ((), (), s32[]{:S(2)}) async-start(), calls=%async_computation.5 | async-start | bytes 8785920 | tf_op jit(solution)/shard_map/all_gather | solution.py:167
  123.3 4.4 %copy-start.2 = (bf16[512,4096]{1,0:T(8,128)(2,1)S(1)}, bf16[512,4096]{1,0:T(8,128)(2,1)}, u32[]{:S(2)}) copy-start(bf16[512,4096]{1,0:T(8,128)(2,1)} %all-gather.4.cloned.1.call-done) | copy-start | bytes 12582916
  127.8 2.6 copy-start.4
  127.8 2.6 copy-start.5
  130.3 159.1 %reduce-scatter.3.cloned.1.call-start = ((), (), s32[]{:S(2)}) async-start(), calls=%async_computation.3 | async-start | bytes 5242880 | tf_op jit(solution)/shard_map/reduce_scatter | solution.py:23
  196.2 3.4 %copy-start.1 = (bf16[33280,128]{1,0:T(8,128)(2,1)S(1)}, bf16[33280,128]{1,0:T(8,128)(2,1)}, u32[]{:S(2)}) copy-start(bf16[33280,128]{1,0:T(8,128)(2,1)} %all-gather.6.cloned.1.call-done) | copy-start | bytes 25559044
  199.6 18.9 %copy-start.6 = (bf16[512,4096]{1,0:T(8,128)(2,1)S(1)}, bf16[512,4096]{1,0:T(8,128)(2,1)}, u32[]{:S(2)}) copy-start(bf16[512,4096]{1,0:T(8,128)(2,1)} %param.13) | copy-start | bytes 12582916
  237.7 94.8 %reduce-scatter.5.cloned.1.call-start = ((), (), s32[]{:S(2)}) async-start(), calls=%async_computation.4 | async-start | bytes 1572864 | tf_op jit(solution)/shard_map/reduce_scatter | solution.py:23
Sparse Core Ops, SparseCore 0:
  9.8 113.4 all-gather.3
  130.4 63.6 all-gather.5
  237.8 51.5 reduce-scatter.2
  291.7 40.7 reduce-scatter.4

commit v2 on v1

v2 whole, which is shorter than its diff:
```python
import jax
import jax.numpy as jnp
from jax import lax
from jax.experimental import pallas as pl
from jax.experimental.pallas import tpu as pltpu
from jax.sharding import Mesh
from jax.sharding import PartitionSpec as P

HD = 128
SPAN = 256
LOG2E = 1.4426950408889634
TP = ("tp_0", "tp_1")
CP = ("cp_0", "cp_1", "cp_2")


theta_base = 500000.0
floor_score = -1e30


MESH = pl.DeviceIdType.MESH
CHUNKS = 4
ROWS = 128
TAG = 2 * ROWS
BLOCK = TAG + 16


def shifted(x=0, y=0, z=0, row=0, other_core=False):
    place = {}
    if x:
        place["tp_1"] = lax.rem(lax.axis_index("tp_1") + x + 4, 4)
    if y:
        place["cp_1"] = lax.rem(lax.axis_index("cp_1") + y + 4, 4)
    if z:
        place["tp_0"] = 1 - lax.axis_index("tp_0")
    if row:
        place["cp_0"] = lax.rem(lax.axis_index("cp_0") + row, 4)
    if other_core:
        place["cp_2"] = 1 - lax.axis_index("cp_2")
    return place


def greet(peers):
    barrier = pltpu.get_barrier_semaphore()
    for peer in peers:
        pl.semaphore_signal(barrier, inc=1, device_id=peer, device_id_type=MESH)
    pl.semaphore_wait(barrier, len(peers))


def send(source, target, sems, index, peer):
    copy = pltpu.make_async_remote_copy(
        src_ref=source,
        dst_ref=target,
        send_sem=sems[0].at[index],
        recv_sem=sems[1].at[index],
        device_id=peer,
        device_id_type=MESH,
    )
    copy.start()
    return copy


def project_kernel(
    ids_ref,
    tokens_ref,
    wq_hbm,
    wk_hbm,
    wv_hbm,
    cos_ref,
    sin_ref,
    q_ref,
    kv_ref,
    wq_ref,
    wk_ref,
    wv_ref,
    held,
    weight_sem,
    token_send,
    token_recv,
    key_send,
    key_recv,
):
    x, zhi = lax.axis_index("tp_1"), lax.axis_index("tp_0")
    row, y, core = lax.axis_index("cp_0"), lax.axis_index("cp_1"), lax.axis_index("cp_2")
    loads = [
        pltpu.make_async_copy(a, b, weight_sem.at[i])
        for i, (a, b) in enumerate(((wk_hbm, wk_ref), (wv_hbm, wv_ref), (wq_hbm, wq_ref)))
    ]
    for load in loads:
        load.start()
    right, left, across = shifted(x=1), shifted(x=-1), shifted(z=1)
    up, down, mate = shifted(y=1), shifted(y=-1), shifted(other_core=True)
    rows_of = [shifted(row=d) for d in (1, 2, 3)]
    greet([right, left, across, up, down, mate] + rows_of)
    tok, key = (token_send, token_recv), (key_send, key_recv)
    sent = []
    half = ROWS // 2

    def token_rows(c, part=None):
        if part is None:
            return pl.ds(c * ROWS, ROWS)
        return pl.ds(c * ROWS + part * half, half)

    def source_of(dz, c):
        if dz == 0:
            return tokens_ref.at[token_rows(c)]
        return held.at[1, 0, token_rows(c)]

    def across_send(c):
        copy = send(
            tokens_ref.at[token_rows(c)], held.at[1, 0, token_rows(c)], tok, c * 9 + 8, across
        )
        sent.append(copy)
        return copy

    def side_sends(c, dz):
        source = source_of(dz, c)
        a = send(source, held.at[dz, 3, token_rows(c)], tok, c * 9 + dz * 4, right)
        b = send(source, held.at[dz, 1, token_rows(c)], tok, c * 9 + dz * 4 + 1, left)
        sent.extend((a, b))
        return a, b

    def side_forwards(c, dz):
        rows = token_rows(c, 0)
        a = send(held.at[dz, 3, rows], held.at[dz, 2, rows], tok, c * 9 + dz * 4 + 2, right)
        rows = token_rows(c, 1)
        b = send(held.at[dz, 1, rows], held.at[dz, 2, rows], tok, c * 9 + dz * 4 + 3, left)
        sent.extend((a, b))
        return a, b

    def weights_at(dz, dx):
        owner = lax.rem(zhi + dz, 2) * 4 + lax.rem(x + dx, 4)
        rows = pl.ds(pl.multiple_of(owner * 512, 512), 512)
        return jnp.concatenate([wk_ref[rows, :], wv_ref[rows, :], wq_ref[rows, :]], axis=1)

    def product(c, dz, dx):
        if dz == 0 and dx == 0:
            features = tokens_ref[token_rows(c), :]
        else:
            features = held[dz, dx, token_rows(c), :]
        return jnp.dot(features, weights_at(dz, dx), preferred_element_type=jnp.float32)

    def group(c, g, b):
        return kv_ref.at[c, g, b]

    def key_rows(c):
        out = []
        for i, peer in enumerate(rows_of):
            block = kv_ref.at[c, core, y, row]
            out.append(send(block, block, key, c * 11 + i, peer))
        sent.extend(out)
        return out

    def key_sides(c, arrivals):
        for copy in arrivals:
            copy.wait_recv()
        mine = group(c, core, y)
        a = send(mine, mine, key, c * 11 + 3, up)
        b = send(mine, mine, key, c * 11 + 4, down)
        m = send(mine, mine, key, c * 11 + 7, mate)
        sent.extend((a, b, m))
        return a, b, m

    def key_forwards(c, sides):
        a, b, m = sides
        a.wait_recv()
        behind = lax.rem(y + 3, 4)
        part = kv_ref.at[c, core, behind, pl.ds(0, 2)]
        fa = send(part, part, key, c * 11 + 5, up)
        got = group(c, core, behind)
        ma = send(got, got, key, c * 11 + 8, mate)
        b.wait_recv()
        ahead = lax.rem(y + 1, 4)
        part = kv_ref.at[c, core, ahead, pl.ds(2, 2)]
        fb = send(part, part, key, c * 11 + 6, down)
        got = group(c, core, ahead)
        mb = send(got, got, key, c * 11 + 9, mate)
        sent.extend((fa, fb, ma, mb))
        return fa, fb, m, ma, mb

    def key_last(c, moved):
        fa, fb, m, ma, mb = moved
        fa.wait_recv()
        fb.wait_recv()
        got = group(c, core, lax.rem(y + 2, 4))
        mc = send(got, got, key, c * 11 + 10, mate)
        sent.append(mc)
        return m, ma, mb, mc

    across_of, own_of, far_of, rows_at, sides_at, moved_at, mates = {}, {}, {}, {}, {}, {}, []
    for c in range(2):
        across_of[c] = across_send(c)
        own_of[c] = side_sends(c, 0)
    across_of[0].wait_recv()
    far_of[0] = side_sends(0, 1)
    for c in range(CHUNKS):
        for copy in own_of[c]:
            copy.wait_recv()
        near = side_forwards(c, 0)
        if c + 2 < CHUNKS:
            across_of[c + 2] = across_send(c + 2)
        if c >= 1:
            sides_at[c - 1] = key_sides(c - 1, rows_at[c - 1])
        for copy in far_of[c]:
            copy.wait_recv()
        far = side_forwards(c, 1)
        if c + 2 < CHUNKS:
            own_of[c + 2] = side_sends(c + 2, 0)
        if c + 1 < CHUNKS:
            across_of[c + 1].wait_recv()
            far_of[c + 1] = side_sends(c + 1, 1)
        if c == 0:
            for load in loads:
                load.wait()
        total = product(c, 0, 0)
        for dz, dx in ((0, 3), (0, 1), (1, 0), (1, 3), (1, 1)):
            total = total + product(c, dz, dx)
        for copy in near:
            copy.wait_recv()
        total = total + product(c, 0, 2)
        for copy in far:
            copy.wait_recv()
        total = total + product(c, 1, 2)
        cosine, sine = cos_ref[token_rows(c), :], sin_ref[token_rows(c), :]

        def turned(vectors):
            return (vectors * cosine + pltpu.roll(vectors, HD // 2, 1) * sine).astype(jnp.bfloat16)

        kv_ref[c, core, y, row, :ROWS, :] = turned(total[:, :HD])
        kv_ref[c, core, y, row, ROWS:TAG, :] = total[:, HD : 2 * HD].astype(jnp.bfloat16)
        tag = ids_ref[0, c // 2].astype(jnp.float32)
        kv_ref[c, core, y, row, TAG:, :] = jnp.full((16, HD), tag, jnp.float32).astype(jnp.bfloat16)
        for head in range(4):
            at = head * SPAN + (c % 2) * ROWS
            q_ref[c // 2, at : at + ROWS, :] = turned(total[:, (2 + head) * HD : (3 + head) * HD])
        rows_at[c] = key_rows(c)
        if c >= 1:
            moved_at[c - 1] = key_forwards(c - 1, sides_at[c - 1])
        if c >= 2:
            mates.extend(key_last(c - 2, moved_at[c - 2]))
    last = CHUNKS - 1
    mates.extend(key_last(last - 1, moved_at[last - 1]))
    sides_at[last] = key_sides(last, rows_at[last])
    moved_at[last] = key_forwards(last, sides_at[last])
    mates.extend(key_last(last, moved_at[last]))
    for copy in mates:
        copy.wait_recv()
    for copy in sent:
        copy.wait_send()


def project(span_ids, tokens, q_weight, k_weight, v_weight, cosine, sine):
    vmem = pl.BlockSpec(memory_space=pltpu.VMEM)
    hbm = pl.BlockSpec(memory_space=pl.ANY)
    return pl.pallas_call(
        project_kernel,
        out_shape=(
            jax.ShapeDtypeStruct((2, 4 * SPAN, HD), jnp.bfloat16),
            jax.ShapeDtypeStruct((CHUNKS, 2, 4, 4, BLOCK, HD), jnp.bfloat16),
        ),
        in_specs=[pl.BlockSpec(memory_space=pltpu.SMEM), vmem, hbm, hbm, hbm, vmem, vmem],
        out_specs=(vmem, vmem),
        scratch_shapes=[
            pltpu.VMEM(q_weight.shape, jnp.bfloat16),
            pltpu.VMEM(k_weight.shape, jnp.bfloat16),
            pltpu.VMEM(v_weight.shape, jnp.bfloat16),
            pltpu.VMEM((2, 4) + tokens.shape, jnp.bfloat16),
            pltpu.SemaphoreType.DMA((3,)),
            pltpu.SemaphoreType.DMA((CHUNKS * 9,)),
            pltpu.SemaphoreType.DMA((CHUNKS * 9,)),
            pltpu.SemaphoreType.DMA((CHUNKS * 11,)),
            pltpu.SemaphoreType.DMA((CHUNKS * 11,)),
        ],
        compiler_params=pltpu.CompilerParams(
            collective_id=0, has_side_effects=True, vmem_limit_bytes=40 * 1024 * 1024
        ),
        name="project",
    )(span_ids, tokens, q_weight, k_weight, v_weight, cosine, sine)


def attend_kernel(info, q_ref, kv_ref, start_ref, out_ref, top_ref, acc_ref):
    heads = q_ref.shape[1] // SPAN
    scale = LOG2E * HD**-0.5
    ones = jnp.ones((SPAN, HD), jnp.bfloat16)

    def block(half, span, masked, first):
        place = info[span]
        first_place = (place // 32) * 64 + place % 32
        places = (first_place, first_place + 32)
        keys = jnp.concatenate([kv_ref[at, :ROWS, :] for at in places], axis=0)
        values = jnp.concatenate([kv_ref[at, ROWS:TAG, :] for at in places], axis=0)
        values = jnp.concatenate([values, ones], axis=1)
        if masked:
            key = span * SPAN + lax.broadcasted_iota(jnp.int32, (SPAN, SPAN), 1)
            start = start_ref[half]
            seen = key >= jnp.concatenate([start, start], axis=1)
            if first:
                query = span * SPAN + lax.broadcasted_iota(jnp.int32, (SPAN, SPAN), 0)
                seen = seen & (key <= query)
        for head in range(heads):
            rows = slice(head * SPAN, (head + 1) * SPAN)
            score = lax.dot_general(
                q_ref[half, rows, :],
                keys,
                (((1,), (1,)), ((), ())),
                preferred_element_type=jnp.float32,
            )
            score = score * scale
            if masked:
                score = jnp.where(seen, score, floor_score)
            top = jnp.max(score, axis=1, keepdims=True)
            if first:
                weight = jnp.exp2(score - top)
                top_ref[rows, :] = jnp.broadcast_to(top, (SPAN, HD))
            else:
                before = top_ref[rows, :]
                now = jnp.maximum(before, top)
                weight = jnp.exp2(score - jnp.concatenate([now, now], axis=1))
                fade = jnp.exp2(before - now)
                top_ref[rows, :] = now
            mixed = jnp.dot(
                weight.astype(jnp.bfloat16), values, preferred_element_type=jnp.float32
            )
            if not first:
                mixed = mixed + acc_ref[rows, :] * jnp.concatenate([fade, fade], axis=1)
            acc_ref[rows, :] = mixed

    for half in range(2):
        own, low, clear = info[64 + half], info[66 + half], info[68 + half]
        block(half, own, True, True)
        lax.fori_loop(low, clear, lambda s, c: (block(half, s, True, False), c)[1], 0)
        lax.fori_loop(clear, own, lambda s, c: (block(half, s, False, False), c)[1], 0)
        for head in range(heads):
            rows = slice(head * SPAN, (head + 1) * SPAN)
            mixed = acc_ref[rows, :HD] / acc_ref[rows, HD:]
            out_ref[half * SPAN : (half + 1) * SPAN, head * HD : (head + 1) * HD] = mixed.astype(
                jnp.bfloat16
            )


def attend(info, queries, gathered, starts):
    vmem = pl.BlockSpec(memory_space=pltpu.VMEM)
    rows = queries.shape[1]
    heads = rows // SPAN
    return pl.pallas_call(
        attend_kernel,
        out_shape=jax.ShapeDtypeStruct((2 * SPAN, heads * HD), jnp.bfloat16),
        in_specs=[pl.BlockSpec(memory_space=pltpu.SMEM), vmem, vmem, vmem],
        out_specs=vmem,
        scratch_shapes=[
            pltpu.VMEM((rows, HD), jnp.float32),
            pltpu.VMEM((rows, 2 * HD), jnp.float32),
        ],
        compiler_params=pltpu.CompilerParams(vmem_limit_bytes=32 * 1024 * 1024),
        name="attend",
    )(info, queries, gathered, starts)


def combine_kernel(
    attn_ref, weight_ref, out_ref, far_out, far_in, near_out, near_in, over_out, over_in, kept,
    send_sem, recv_sem,
):
    x, zhi = lax.axis_index("tp_1"), lax.axis_index("tp_0")
    right, left, across = shifted(x=1), shifted(x=-1), shifted(z=1)
    greet([right, left, across])
    sems = (send_sem, recv_sem)
    steps = kept.shape[0]
    size = kept.shape[1]
    half = size // 2
    width = out_ref.shape[1]
    sent = []

    def share(c, dx):
        rows = attn_ref[c * size : (c + 1) * size, :]
        terms = []
        for dz in range(2):
            owner = lax.rem(zhi + dz, 2) * 4 + lax.rem(x + dx, 4)
            columns = pl.ds(pl.multiple_of(owner * width, width), width)
            terms.append(
                jnp.dot(rows, weight_ref[:, columns], preferred_element_type=jnp.float32)
            )
        return jnp.concatenate(terms, axis=1)

    def open_step(c):
        far = share(c, 2).astype(jnp.bfloat16)
        far_out[c, 0] = far[:half]
        far_out[c, 1] = far[half:]
        a = send(far_out.at[c, 0], far_in.at[c, 0], sems, c * 7, right)
        b = send(far_out.at[c, 1], far_in.at[c, 1], sems, c * 7 + 1, left)
        to_right, to_left = share(c, 1), share(c, 3)
        near_out[c, 0, 1] = to_right[half:].astype(jnp.bfloat16)
        d = send(near_out.at[c, 0, 1], near_in.at[c, 0, 1], sems, c * 7 + 2, right)
        near_out[c, 1, 0] = to_left[:half].astype(jnp.bfloat16)
        e = send(near_out.at[c, 1, 0], near_in.at[c, 1, 0], sems, c * 7 + 3, left)
        near_out[c, 0, 0] = to_right[:half].astype(jnp.bfloat16)
        near_out[c, 1, 1] = to_left[half:].astype(jnp.bfloat16)
        sent.extend((a, b, d, e))
        return a, b, d, e

    def pass_on(c, opened):
        a, b, d, e = opened
        a.wait_recv()
        near_out[c, 0, 0] = (
            near_out[c, 0, 0].astype(jnp.float32) + far_in[c, 0].astype(jnp.float32)
        ).astype(jnp.bfloat16)
        f = send(near_out.at[c, 0, 0], near_in.at[c, 0, 0], sems, c * 7 + 4, right)
        b.wait_recv()
        near_out[c, 1, 1] = (
            near_out[c, 1, 1].astype(jnp.float32) + far_in[c, 1].astype(jnp.float32)
        ).astype(jnp.bfloat16)
        g = send(near_out.at[c, 1, 1], near_in.at[c, 1, 1], sems, c * 7 + 5, left)
        sent.extend((f, g))
        return d, e, f, g

    def cross(c, passed):
        total = share(c, 0)
        for copy in passed:
            copy.wait_recv()
        for side in range(2):
            both = jnp.concatenate([near_in[c, side, 0], near_in[c, side, 1]], axis=0)
            total = total + both.astype(jnp.float32)
        over_out[c] = total[:, width:].astype(jnp.bfloat16)
        kept[c] = total[:, :width]
        copy = send(over_out.at[c], over_in.at[c], sems, c * 7 + 6, across)
        sent.append(copy)
        return copy

    def close(c, crossed):
        crossed.wait_recv()
        out_ref[c * size : (c + 1) * size, :] = (
            kept[c] + over_in[c].astype(jnp.float32)
        ).astype(jnp.bfloat16)

    opened, passed, crossed = {}, {}, {}
    for c in range(2):
        opened[c] = open_step(c)
    for c in range(steps):
        passed[c] = pass_on(c, opened[c])
        if c + 2 < steps:
            opened[c + 2] = open_step(c + 2)
        if c >= 1:
            crossed[c - 1] = cross(c - 1, passed[c - 1])
        if c >= 2:
            close(c - 2, crossed[c - 2])
    crossed[steps - 1] = cross(steps - 1, passed[steps - 1])
    close(steps - 2, crossed[steps - 2])
    close(steps - 1, crossed[steps - 1])
    for copy in sent:
        copy.wait_send()


STEPS = 4


def combine(attention, o_weight):
    vmem = pl.BlockSpec(memory_space=pltpu.VMEM)
    rows, width = attention.shape[0], o_weight.shape[1] // 8
    size = rows // STEPS
    half = (size // 2, 2 * width)
    return pl.pallas_call(
        combine_kernel,
        out_shape=jax.ShapeDtypeStruct((rows, width), jnp.bfloat16),
        in_specs=[vmem, vmem],
        out_specs=vmem,
        scratch_shapes=[
            pltpu.VMEM((STEPS, 2) + half, jnp.bfloat16),
            pltpu.VMEM((STEPS, 2) + half, jnp.bfloat16),
            pltpu.VMEM((STEPS, 2, 2) + half, jnp.bfloat16),
            pltpu.VMEM((STEPS, 2, 2) + half, jnp.bfloat16),
            pltpu.VMEM((STEPS, size, width), jnp.bfloat16),
            pltpu.VMEM((STEPS, size, width), jnp.bfloat16),
            pltpu.VMEM((STEPS, size, width), jnp.float32),
            pltpu.SemaphoreType.DMA((STEPS * 7,)),
            pltpu.SemaphoreType.DMA((STEPS * 7,)),
        ],
        compiler_params=pltpu.CompilerParams(
            collective_id=1, has_side_effects=True, vmem_limit_bytes=32 * 1024 * 1024
        ),
        name="combine",
    )(attention, o_weight)


def plan(span_table, own, starts):
    blocks = jnp.arange(64, dtype=jnp.int32)
    where = jnp.sum(
        jnp.where(span_table.reshape(1, 64) == blocks[:, None], blocks[None, :], 0), axis=1
    )
    low = starts[:, 0] // SPAN
    clear = jnp.minimum((starts[:, -1] + SPAN - 1) // SPAN, own)
    return jnp.concatenate([where, own, low, clear, jnp.zeros(58, jnp.int32)])


def turn_tables(positions):
    half_size = HD // 2
    exponent = jnp.arange(half_size, dtype=jnp.float32) * (2.0 / HD)
    inverse_freq = theta_base ** (-exponent)
    angles = positions.astype(jnp.float32)[:, None] * inverse_freq[None, :]
    cosine, sine = jnp.cos(angles), jnp.sin(angles)
    return jnp.concatenate([cosine, cosine], axis=1), jnp.concatenate([-sine, sine], axis=1)


def per_device(tokens, span_ids, positions, q_weight, k_weight, v_weight, o_weight):
    cosine, sine = turn_tables(positions)
    queries, held = project(span_ids, tokens, q_weight, k_weight, v_weight, cosine, sine)
    span_table = held[::2, :, :, :, TAG, 0].astype(jnp.int32)
    own = span_ids.reshape(2)
    offsets = jnp.arange(SPAN, dtype=jnp.int32)
    starts = own[:, None] * SPAN + offsets[None, :] - positions.reshape(2, SPAN)
    info = plan(span_table, own, starts)
    starts = jnp.broadcast_to(starts[:, :, None], (2, SPAN, HD))
    attention = attend(info, queries, held.reshape(-1, BLOCK, HD), starts)
    return combine(attention, o_weight)


def solution(mesh):
    split = Mesh(mesh.devices.reshape(4, 4, 2, 2, 4), ("cp_0", "cp_1", "cp_2", "tp_0", "tp_1"))
    placed = (P(CP, TP), P(CP, None), P(CP), P(None, TP), P(None, TP), P(None, TP), P(TP, None))
    return jax.shard_map(
        per_device, mesh=split, in_specs=placed, out_specs=P(CP, TP), check_vma=False
    )
```

time: 341 us -> 179 us (0.52)
  the two profiles are of different devices: /device:TPU:16 before, /device:TPU:88 now
where the time goes in v2:
time: 179 us
  Pallas kernels  164 us (92%)
  local copies, waits for them, and re-layouts  11 us (6%)
  other arithmetic  4.51 us (3%)
    pallas_call x1, Pallas kernels, project(): pl.pallas_call(project_kernel, out_shape=(jax.ShapeDtypeStruct((2, 4 * SP...  87.4 us
    pallas_call x1, Pallas kernels, combine(): pl.pallas_call(combine_kernel, out_shape=jax.ShapeDtypeStruct((rows, widt...  54.2 us
    pallas_call x1, Pallas kernels, attend(): pl.pallas_call(attend_kernel, out_shape=jax.ShapeDtypeStruct((2 * SPAN, h...  22 us
    unnamed x19, local copies, waits for them, and re-layouts  10.7 us

profile of v2, /device:TPU:88, one launch (start us, length us, event | category | flops | bytes accessed | tf_op | source)
XLA Modules:
  0.0 179.3 jit_solution(5726698417158462701)
XLA Ops:
  0.0 0.8 convert_element_type.13
  0.8 1.0 fusion
  1.8 0.2 pad_maximum_fusion
  2.0 0.0 copy-start.2
  2.0 2.2 %copy-done.2 = bf16[4096,512]{1,0:T(8,128)(2,1)S(1)} copy-done((bf16[4096,512]{1,0:T(8,128)(2,1)S(1)}, bf16[4096,512]{1,0:T(8,128)(2,1)}, u32[]{:S(2)}) %copy-start.2) | copy-done | bytes 4194328
  4.2 1.2 copy-done.3
  5.4 1.2 copy-done.4
  6.6 1.0 copy-done.5
  7.7 0.7 copy-done.6
  8.3 87.4 %project.1 = (bf16[2,1024,128]{2,1,0:T(8,128)(2,1)S(1)}, bf16[4,2,4,4,272,128]{5,4,3,2,1,0:T(8,128)(2,1)}) custom-call(s32[1,2]{1,0:T(1,128)S(1)} %copy-done.6, bf16[512,512]{1,0:T(8,128)(2,1)S(1)} %copy-done.5, bf16[4096,512]{1,0:T(8,128)(2,1)S(1)} %copy-done.2, bf16[4096,128]{1,0:T(8,128)(2,1)S(1)} %copy-done.3, bf16[4096,128]{1,0:T(8,128)(2,1)S(1)} %copy-done.4, ...), custom_call_target="tpu_custom_call" | custom-call | tf_op jit(solution)/shard_map/project/pallas_call | solution.py:254
  95.8 2.2 %convert_reduce_fusion = s32[2,2,4,4]{3,2,1,0:T(4,128)S(1)} fusion(bf16[4,2,4,4,272,128]{5,4,3,2,1,0:T(8,128)(2,1)} %get-tuple-element.7), kind=kLoop, calls=%fused_computation.5 | loop fusion | flops 64 | bytes 384 | tf_op jit(solution)/shard_map/convert_element_type | solution.py:504
  97.9 0.1 reshape.61
  98.0 0.1 select_reduce_fusion
  98.1 0.0 copy-done.8
  98.2 0.0 copy-done.7
  98.2 0.1 add_subtract_fusion
  98.3 0.2 fusion.1
  98.5 0.1 concatenate.11.info
  98.6 0.1 broadcast_in_dim.29.start_ref
  98.7 0.0 copy-start
  98.7 3.5 %copy-done = bf16[4,2,4,4,272,128]{5,4,3,2,1,0:T(8,128)(2,1)S(1)} copy-done((bf16[4,2,4,4,272,128]{5,4,3,2,1,0:T(8,128)(2,1)S(1)}, bf16[4,2,4,4,272,128]{5,4,3,2,1,0:T(8,128)(2,1)}, u32[]{:S(2)}) %copy-start) | copy-done | bytes 8912920
  102.2 22.0 %attend.1.attn_ref = bf16[512,512]{1,0:T(8,128)(2,1)S(1)} custom-call(s32[128]{0:T(128)S(1)} %concatenate.11.info, bf16[2,1024,128]{2,1,0:T(8,128)(2,1)S(1)} %get-tuple-element.8.q_ref, bf16[128,272,128]{2,1,0:T(8,128)(2,1)S(1)} %bitcast.4, s32[2,256,128]{2,1,0:T(8,128)S(1)} %broadcast_in_dim.29.start_ref), custom_call_target="tpu_custom_call" | custom-call | tf_op jit(solution)/shard_map/attend/pallas_call | solution.py:344
  124.2 54.2 %combine.1 = bf16[512,512]{1,0:T(8,128)(2,1)S(1)} custom-call(bf16[512,512]{1,0:T(8,128)(2,1)S(1)} %attend.1.attn_ref, bf16[512,4096]{1,0:T(8,128)(2,1)S(1)} %copy-done.1), custom_call_target="tpu_custom_call" | custom-call | tf_op jit(solution)/shard_map/combine/pallas_call | solution.py:459
  178.5 0.8 copy.10
  (13 shorter events, 0.1 us)
Async XLA Ops:
  0.0 98.1 %copy-start.8 = (s32[512]{0:T(512)S(1)}, s32[512]{0:T(512)}, u32[]{:S(2)}) copy-start(s32[512]{0:T(512)} %param.9) | copy-start | bytes 6148
  0.0 98.2 %copy-start.7 = (s32[1,2]{1,0:T(1,128)S(1)}, s32[1,2]{1,0:T(1,128)}, u32[]{:S(2)}) copy-start(s32[1,2]{1,0:T(1,128)} %ids_ref.1) | copy-start | bytes 28
  2.0 2.2 %copy-start.2 = (bf16[4096,512]{1,0:T(8,128)(2,1)S(1)}, bf16[4096,512]{1,0:T(8,128)(2,1)}, u32[]{:S(2)}) copy-start(bf16[4096,512]{1,0:T(8,128)(2,1)} %wq_hbm.1) | copy-start | bytes 12582916
  4.2 1.2 copy-start.3
  5.4 1.2 copy-start.4
  6.6 1.0 copy-start.5
  7.7 0.7 copy-start.6
  98.7 3.5 %copy-start = (bf16[4,2,4,4,272,128]{5,4,3,2,1,0:T(8,128)(2,1)S(1)}, bf16[4,2,4,4,272,128]{5,4,3,2,1,0:T(8,128)(2,1)}, u32[]{:S(2)}) copy-start(bf16[4,2,4,4,272,128]{5,4,3,2,1,0:T(8,128)(2,1)} %get-tuple-element.7) | copy-start | bytes 26738692
  102.2 22.0 %copy-start.1 = (bf16[512,4096]{1,0:T(8,128)(2,1)S(1)}, bf16[512,4096]{1,0:T(8,128)(2,1)}, u32[]{:S(2)}) copy-start(bf16[512,4096]{1,0:T(8,128)(2,1)} %weight_ref.1) | copy-start | bytes 12582916
